TPU v7x, 32 devices: a whole 2x2x4 slice. The times are simulated.
32 devices in a mesh: prow: 4 (over z), pcol: 8 (over y, x, core).
Axes of the slice: x: 2, y: 2, z: 4, core: 2. Of those that a mesh axis runs over, the one named last changes fastest.
Arguments:
- ainv_in: float32 [36, 4, 18, 8, 128, 128], P(None, 'prow', None, 'pcol'), as said below
- ufactor: bfloat16 [36, 4, 6, 128, 128], P(None, 'prow'), may hold values from -0.08984375 to 0.08984375
- dinv: float32 [6, 128, 128], replicated, may hold values from -6 to 6
- pattern: int32 [144, 144], replicated, may hold values from 0 to 1, as said below
Outputs:
- ainv_out: float32 [36, 4, 18, 8, 128, 128], P(None, 'prow', None, 'pcol')
Inputs may be any that keep to these rules, and one draw needn't show every extreme that they name: For a column j below 6, pattern[i, j] is 0 for i <= j, 1 at the parent row (the nearest row below j that has a 1, at most 3 below j), and the other 1s of column j lie in rows where the parent's column has a 1; for j at least 6, pattern[i, j] is 1 exactly where i > j. `ainv_in`: a symmetric matrix.
All inputs are finite; a program needn't handle non-finite values.
Results may differ from a plain program's by a relative error of at most 0.0003.
Values may be sent and summed in bfloat16 or wider, within the bound.
A program may use at most 192 MiB of HBM per device.

v0:
```python
import jax
import jax.numpy as jnp
from jax import lax
from jax.sharding import PartitionSpec as P


def spread(value, axis, source):
    kept = jnp.where(lax.axis_index(axis) == source, value, 0).astype(value.dtype)
    return lax.psum(kept, axis)


def per_device(ainv_in, ufactor, dinv, pattern):
    row_blocks, _, col_blocks, _, width, _ = ainv_in.shape
    step_count = dinv.shape[0]
    blocks = ainv_in.reshape(row_blocks, col_blocks, width, width)
    lower = ufactor.reshape(row_blocks, step_count, width, width)
    row_count = lax.axis_size("prow")
    col_count = lax.axis_size("pcol")
    prow_id = lax.axis_index("prow")
    pcol_id = lax.axis_index("pcol")
    row_ids = jnp.arange(row_blocks, dtype=jnp.int32) * row_count + prow_id
    col_ids = jnp.arange(col_blocks, dtype=jnp.int32) * col_count + pcol_id
    fold_ratio = col_count // row_count
    pick_slot = pcol_id // row_count
    home_row = pcol_id % row_count
    mask_rows = pattern[row_ids, :]
    live_lower = mask_rows[:, :step_count] > 0
    masked_lower = jnp.where(live_lower[:, :, None, None], lower, jnp.zeros_like(lower))
    chosen_cols = lax.dynamic_index_in_dim(
        masked_lower.reshape(col_blocks, fold_ratio, step_count, width, width),
        pick_slot,
        1,
        keepdims=False,
    )
    other_cols = spread(chosen_cols, "prow", home_row)

    def fetch(column):
        own_col = lax.dynamic_index_in_dim(masked_lower, column, 1, keepdims=False)
        other_rows = lax.dynamic_index_in_dim(other_cols, column, 1, keepdims=False)
        return (own_col, other_rows)

    def advance(taken, matrix):
        column = step_count - 1 - taken
        own_col, other_rows = fetch(column)
        partial_value = -jnp.einsum(
            "acxy,cyz->axz", matrix, other_rows.astype(jnp.float32), precision=lax.Precision.HIGHEST
        )
        col_piece = lax.psum_scatter(partial_value, "pcol", scatter_dimension=1, tiled=True)
        col_whole = lax.all_gather(col_piece, "pcol", axis=1, tiled=True)
        live_rows = lax.dynamic_index_in_dim(mask_rows, column, 1, keepdims=False) > 0
        inverse_col = jnp.where(live_rows[:, None, None], col_whole, jnp.zeros_like(col_whole))
        diag_term = jnp.einsum(
            "axy,axz->yz", own_col.astype(jnp.float32), inverse_col, precision=lax.Precision.HIGHEST
        )
        diag_total = lax.psum(diag_term, "prow")
        diag_block = lax.dynamic_index_in_dim(dinv, column, 0, keepdims=False) - diag_total
        new_col = jnp.where((row_ids == column)[:, None, None], diag_block[None], inverse_col)
        col_slot = column // col_count
        old_col = lax.dynamic_index_in_dim(matrix, col_slot, 1, keepdims=False)
        matrix = lax.dynamic_update_index_in_dim(
            matrix, jnp.where(pcol_id == column % col_count, new_col, old_col), col_slot, 1
        )
        chosen = lax.dynamic_index_in_dim(
            inverse_col.reshape(col_blocks, fold_ratio, width, width), pick_slot, 1, keepdims=False
        )
        across = spread(chosen, "prow", home_row)
        row_vals = jnp.where((col_ids == column)[:, None, None], diag_block[None], across)
        row_vals = jnp.swapaxes(row_vals, 1, 2)
        row_slot = column // row_count
        old_row = lax.dynamic_index_in_dim(matrix, row_slot, 0, keepdims=False)
        matrix = lax.dynamic_update_index_in_dim(
            matrix, jnp.where(prow_id == column % row_count, row_vals, old_row), row_slot, 0
        )
        return matrix

    blocks = lax.fori_loop(0, step_count, advance, blocks)
    return blocks.reshape(ainv_in.shape)


def solution(mesh):
    placed = (
        P(None, "prow", None, "pcol", None, None),
        P(None, "prow", None, None, None),
        P(),
        P(),
    )
    return jax.shard_map(
        per_device,
        mesh=mesh,
        in_specs=placed,
        out_specs=P(None, "prow", None, "pcol", None, None),
        check_vma=False,
    )
```

profile of v0, /device:TPU:0, one launch (start us, length us, event | category | flops | bytes accessed | tf_op | source)
XLA Modules:
  0.0 1241.6 jit_solution(2986418367816600455)
XLA Ops:
  6.5 30.5 %copy.57 = f32[36,1,18,1,128,128]{5,4,3,2,1,0:T(8,128)} copy(f32[36,1,18,1,128,128]{5,4,3,2,1,0:T(8,128)} %param.6) | data formatting | bytes 84934656
  37.8 4.3 fusion.16
  42.2 10.4 copy.31
  52.7 6.5 bitcast_select_fusion.2
  59.1 119.6 %all-reduce.6.cloned.1.call-done = bf16[18,6,128,128]{3,2,1,0:T(8,128)(2,1)} async-done(((bf16[18,6,128,128]{3,2,1,0:T(8,128)(2,1)}), bf16[18,6,128,128]{3,2,1,0:T(8,128)(2,1)}) %all-reduce.6.cloned.1.call-update) | async-done | bytes 3538960 | tf_op jit(solution)/shard_map/psum | solution.py:9
  178.7 1055.4 %while.18 = (s32[]{:T(128)}, f32[36,18,128,128]{3,2,1,0:T(8,128)}, s32[]{:T(128)}, f32[6,128,128]{2,1,0:T(8,128)}, bf16[36,6,128,128]{2,3,0,1:T(8,128)(2,1)}, /*...) while((s32[]{:T(128)}, f32[36,18,128,128]{3,2,1,0:T(8,128)}, ...), condition=%wide.region_5.6_spmd.clone.clone, body=%wide.region_1.5_spmd.clone.clone.sunk | while | flops 17217585152 | bytes 122127656 | solution.py:76
  178.7 27.0 %fusion.30 = f32[36,128,128]{1,2,0:T(8,128)S(1)} fusion(f32[36,18,128,128]{3,2,1,0:T(8,128)} %get-tuple-element.557, bf16[18,6,128,128]{3,2,1,0:T(8,128)(2,1)} %get-tuple-element.586, s32[]{:T(128)S(6)} %select_n.384), kind=kOutput, calls=%fused_computation.6.clone.1 | convolution fusion | flops 16308043776 | bytes 45416452 | tf_op jit(solution)/shard_map/while/body/eval_jaxpr/acxy,cyz->axz/dot_general | solution.py:45
  208.1 42.6 %reduce-scatter.2.cloned.1.call-done = f32[36,16,128]{2,0,1:T(8,128)} async-done(((f32[36,128,128]{2,0,1:T(8,128)}), f32[36,16,128]{2,0,1:T(8,128)}) %reduce-scatter.2.cloned.1.call-update) | async-done | bytes 294928 | tf_op jit(solution)/shard_map/while/body/eval_jaxpr/reduce_scatter | solution.py:48
  252.6 29.3 %all-gather.2.cloned.1.call-done = f32[36,128,128]{2,1,0:T(8,128)} async-done(((f32[36,16,128]{2,1,0:T(8,128)}), f32[36,128,128]{2,1,0:T(8,128)}) %all-gather.2.cloned.1.call-update) | async-done | bytes 2359312 | tf_op jit(solution)/shard_map/while/body/eval_jaxpr/all_gather | solution.py:49
  292.3 54.6 %all-reduce.8.cloned.1.call-done = (f32[128,128]{1,0:T(8,128)}, f32[18,128,128]{1,2,0:T(8,128)}) async-done(((f32[128,128]{1,0:T(8,128)}, f32[18,128,128]{1,2,0:T(8,128)}), (f32[128,128]{1,0:T(8,128)}, f32[18,128,128]{1,2,0:T(8,128)})) %all-reduce.8.cloned.1.call-update) | async-done | bytes 1245200 | tf_op jit(solution)/shard_map/while/body/eval_jaxpr/psum | solution.py:55
  347.9 3.5 bitcast_dynamic-update-slice_fusion.4
  354.2 27.0 %fusion.30 = f32[36,128,128]{1,2,0:T(8,128)S(1)} fusion(f32[36,18,128,128]{3,2,1,0:T(8,128)} %get-tuple-element.557, bf16[18,6,128,128]{3,2,1,0:T(8,128)(2,1)} %get-tuple-element.586, s32[]{:T(128)S(6)} %select_n.384), kind=kOutput, calls=%fused_computation.6.clone.1 | convolution fusion | flops 16308043776 | bytes 45416452 | tf_op jit(solution)/shard_map/while/body/eval_jaxpr/acxy,cyz->axz/dot_general | solution.py:45
  383.6 43.1 %reduce-scatter.2.cloned.1.call-done = f32[36,16,128]{2,0,1:T(8,128)} async-done(((f32[36,128,128]{2,0,1:T(8,128)}), f32[36,16,128]{2,0,1:T(8,128)}) %reduce-scatter.2.cloned.1.call-update) | async-done | bytes 294928 | tf_op jit(solution)/shard_map/while/body/eval_jaxpr/reduce_scatter | solution.py:48
  428.6 29.3 %all-gather.2.cloned.1.call-done = f32[36,128,128]{2,1,0:T(8,128)} async-done(((f32[36,16,128]{2,1,0:T(8,128)}), f32[36,128,128]{2,1,0:T(8,128)}) %all-gather.2.cloned.1.call-update) | async-done | bytes 2359312 | tf_op jit(solution)/shard_map/while/body/eval_jaxpr/all_gather | solution.py:49
  468.3 54.6 %all-reduce.8.cloned.1.call-done = (f32[128,128]{1,0:T(8,128)}, f32[18,128,128]{1,2,0:T(8,128)}) async-done(((f32[128,128]{1,0:T(8,128)}, f32[18,128,128]{1,2,0:T(8,128)}), (f32[128,128]{1,0:T(8,128)}, f32[18,128,128]{1,2,0:T(8,128)})) %all-reduce.8.cloned.1.call-update) | async-done | bytes 1245200 | tf_op jit(solution)/shard_map/while/body/eval_jaxpr/psum | solution.py:55
  530.2 27.1 %fusion.30 = f32[36,128,128]{1,2,0:T(8,128)S(1)} fusion(f32[36,18,128,128]{3,2,1,0:T(8,128)} %get-tuple-element.557, bf16[18,6,128,128]{3,2,1,0:T(8,128)(2,1)} %get-tuple-element.586, s32[]{:T(128)S(6)} %select_n.384), kind=kOutput, calls=%fused_computation.6.clone.1 | convolution fusion | flops 16308043776 | bytes 45416452 | tf_op jit(solution)/shard_map/while/body/eval_jaxpr/acxy,cyz->axz/dot_general | solution.py:45
  559.6 43.1 %reduce-scatter.2.cloned.1.call-done = f32[36,16,128]{2,0,1:T(8,128)} async-done(((f32[36,128,128]{2,0,1:T(8,128)}), f32[36,16,128]{2,0,1:T(8,128)}) %reduce-scatter.2.cloned.1.call-update) | async-done | bytes 294928 | tf_op jit(solution)/shard_map/while/body/eval_jaxpr/reduce_scatter | solution.py:48
  604.6 29.3 %all-gather.2.cloned.1.call-done = f32[36,128,128]{2,1,0:T(8,128)} async-done(((f32[36,16,128]{2,1,0:T(8,128)}), f32[36,128,128]{2,1,0:T(8,128)}) %all-gather.2.cloned.1.call-update) | async-done | bytes 2359312 | tf_op jit(solution)/shard_map/while/body/eval_jaxpr/all_gather | solution.py:49
  644.3 54.6 %all-reduce.8.cloned.1.call-done = (f32[128,128]{1,0:T(8,128)}, f32[18,128,128]{1,2,0:T(8,128)}) async-done(((f32[128,128]{1,0:T(8,128)}, f32[18,128,128]{1,2,0:T(8,128)}), (f32[128,128]{1,0:T(8,128)}, f32[18,128,128]{1,2,0:T(8,128)})) %all-reduce.8.cloned.1.call-update) | async-done | bytes 1245200 | tf_op jit(solution)/shard_map/while/body/eval_jaxpr/psum | solution.py:55
  706.2 27.0 %fusion.30 = f32[36,128,128]{1,2,0:T(8,128)S(1)} fusion(f32[36,18,128,128]{3,2,1,0:T(8,128)} %get-tuple-element.557, bf16[18,6,128,128]{3,2,1,0:T(8,128)(2,1)} %get-tuple-element.586, s32[]{:T(128)S(6)} %select_n.384), kind=kOutput, calls=%fused_computation.6.clone.1 | convolution fusion | flops 16308043776 | bytes 45416452 | tf_op jit(solution)/shard_map/while/body/eval_jaxpr/acxy,cyz->axz/dot_general | solution.py:45
  735.6 43.1 %reduce-scatter.2.cloned.1.call-done = f32[36,16,128]{2,0,1:T(8,128)} async-done(((f32[36,128,128]{2,0,1:T(8,128)}), f32[36,16,128]{2,0,1:T(8,128)}) %reduce-scatter.2.cloned.1.call-update) | async-done | bytes 294928 | tf_op jit(solution)/shard_map/while/body/eval_jaxpr/reduce_scatter | solution.py:48
  780.6 29.3 %all-gather.2.cloned.1.call-done = f32[36,128,128]{2,1,0:T(8,128)} async-done(((f32[36,16,128]{2,1,0:T(8,128)}), f32[36,128,128]{2,1,0:T(8,128)}) %all-gather.2.cloned.1.call-update) | async-done | bytes 2359312 | tf_op jit(solution)/shard_map/while/body/eval_jaxpr/all_gather | solution.py:49
  820.2 54.6 %all-reduce.8.cloned.1.call-done = (f32[128,128]{1,0:T(8,128)}, f32[18,128,128]{1,2,0:T(8,128)}) async-done(((f32[128,128]{1,0:T(8,128)}, f32[18,128,128]{1,2,0:T(8,128)}), (f32[128,128]{1,0:T(8,128)}, f32[18,128,128]{1,2,0:T(8,128)})) %all-reduce.8.cloned.1.call-update) | async-done | bytes 1245200 | tf_op jit(solution)/shard_map/while/body/eval_jaxpr/psum | solution.py:55
  882.2 27.0 %fusion.30 = f32[36,128,128]{1,2,0:T(8,128)S(1)} fusion(f32[36,18,128,128]{3,2,1,0:T(8,128)} %get-tuple-element.557, bf16[18,6,128,128]{3,2,1,0:T(8,128)(2,1)} %get-tuple-element.586, s32[]{:T(128)S(6)} %select_n.384), kind=kOutput, calls=%fused_computation.6.clone.1 | convolution fusion | flops 16308043776 | bytes 45416452 | tf_op jit(solution)/shard_map/while/body/eval_jaxpr/acxy,cyz->axz/dot_general | solution.py:45
  911.6 43.1 %reduce-scatter.2.cloned.1.call-done = f32[36,16,128]{2,0,1:T(8,128)} async-done(((f32[36,128,128]{2,0,1:T(8,128)}), f32[36,16,128]{2,0,1:T(8,128)}) %reduce-scatter.2.cloned.1.call-update) | async-done | bytes 294928 | tf_op jit(solution)/shard_map/while/body/eval_jaxpr/reduce_scatter | solution.py:48
  956.5 29.3 %all-gather.2.cloned.1.call-done = f32[36,128,128]{2,1,0:T(8,128)} async-done(((f32[36,16,128]{2,1,0:T(8,128)}), f32[36,128,128]{2,1,0:T(8,128)}) %all-gather.2.cloned.1.call-update) | async-done | bytes 2359312 | tf_op jit(solution)/shard_map/while/body/eval_jaxpr/all_gather | solution.py:49
  996.2 54.6 %all-reduce.8.cloned.1.call-done = (f32[128,128]{1,0:T(8,128)}, f32[18,128,128]{1,2,0:T(8,128)}) async-done(((f32[128,128]{1,0:T(8,128)}, f32[18,128,128]{1,2,0:T(8,128)}), (f32[128,128]{1,0:T(8,128)}, f32[18,128,128]{1,2,0:T(8,128)})) %all-reduce.8.cloned.1.call-update) | async-done | bytes 1245200 | tf_op jit(solution)/shard_map/while/body/eval_jaxpr/psum | solution.py:55
  1058.2 27.0 %fusion.30 = f32[36,128,128]{1,2,0:T(8,128)S(1)} fusion(f32[36,18,128,128]{3,2,1,0:T(8,128)} %get-tuple-element.557, bf16[18,6,128,128]{3,2,1,0:T(8,128)(2,1)} %get-tuple-element.586, s32[]{:T(128)S(6)} %select_n.384), kind=kOutput, calls=%fused_computation.6.clone.1 | convolution fusion | flops 16308043776 | bytes 45416452 | tf_op jit(solution)/shard_map/while/body/eval_jaxpr/acxy,cyz->axz/dot_general | solution.py:45
  1087.5 43.1 %reduce-scatter.2.cloned.1.call-done = f32[36,16,128]{2,0,1:T(8,128)} async-done(((f32[36,128,128]{2,0,1:T(8,128)}), f32[36,16,128]{2,0,1:T(8,128)}) %reduce-scatter.2.cloned.1.call-update) | async-done | bytes 294928 | tf_op jit(solution)/shard_map/while/body/eval_jaxpr/reduce_scatter | solution.py:48
  1132.5 29.3 %all-gather.2.cloned.1.call-done = f32[36,128,128]{2,1,0:T(8,128)} async-done(((f32[36,16,128]{2,1,0:T(8,128)}), f32[36,128,128]{2,1,0:T(8,128)}) %all-gather.2.cloned.1.call-update) | async-done | bytes 2359312 | tf_op jit(solution)/shard_map/while/body/eval_jaxpr/all_gather | solution.py:49
  1172.2 54.6 %all-reduce.8.cloned.1.call-done = (f32[128,128]{1,0:T(8,128)}, f32[18,128,128]{1,2,0:T(8,128)}) async-done(((f32[128,128]{1,0:T(8,128)}, f32[18,128,128]{1,2,0:T(8,128)}), (f32[128,128]{1,0:T(8,128)}, f32[18,128,128]{1,2,0:T(8,128)})) %all-reduce.8.cloned.1.call-update) | async-done | bytes 1245200 | tf_op jit(solution)/shard_map/while/body/eval_jaxpr/psum | solution.py:55
  1227.8 3.5 bitcast_dynamic-update-slice_fusion.4
  (168 shorter events, 125.0 us)
Async XLA Ops:
  6.5 30.6 %copy-start = (s32[144,144]{1,0:T(8,128)S(1)}, s32[144,144]{1,0:T(8,128)}, u32[]{:S(2)}) copy-start(s32[144,144]{1,0:T(8,128)} %param.9) | copy-start | bytes 248836
  6.5 172.2 %all-reduce.6.cloned.1.call-start = ((), (), s32[]{:S(2)}) async-start(), calls=%async_computation.1 | async-start | bytes 7077888 | tf_op jit(solution)/shard_map/psum | solution.py:9
  178.7 72.0 %reduce-scatter.2.cloned.1.call-start = ((), (), s32[]{:S(2)}) async-start(), calls=%async_computation.2 | async-start | bytes 2949120 | tf_op jit(solution)/shard_map/while/body/eval_jaxpr/reduce_scatter | solution.py:48
  208.1 73.9 %all-gather.2.cloned.1.call-start = ((), (), s32[]{:S(2)}) async-start(), calls=%async_computation.3 | async-start | bytes 2654208 | tf_op jit(solution)/shard_map/while/body/eval_jaxpr/all_gather | solution.py:49
  252.5 94.4 %all-reduce.8.cloned.1.call-start = ((), (), s32[]{:S(2)}) async-start(), calls=%async_computation.4 | async-start | bytes 2490368 | tf_op jit(solution)/shard_map/while/body/eval_jaxpr/psum | solution.py:55
  288.8 59.1 %copy-start.2 = (f32[36,128,128]{2,1,0:T(8,128)S(1)}, f32[36,128,128]{2,1,0:T(8,128)}, u32[]{:S(2)}) copy-start(f32[36,128,128]{2,1,0:T(8,128)} %all-gather.2.cloned.1.call-done) | copy-start | bytes 7077892 | tf_op jit(solution)/shard_map/while
  351.4 1.6 copy-start.3
  354.2 72.5 %reduce-scatter.2.cloned.1.call-start = ((), (), s32[]{:S(2)}) async-start(), calls=%async_computation.2 | async-start | bytes 2949120 | tf_op jit(solution)/shard_map/while/body/eval_jaxpr/reduce_scatter | solution.py:48
  383.6 74.3 %all-gather.2.cloned.1.call-start = ((), (), s32[]{:S(2)}) async-start(), calls=%async_computation.3 | async-start | bytes 2654208 | tf_op jit(solution)/shard_map/while/body/eval_jaxpr/all_gather | solution.py:49
  428.5 94.4 %all-reduce.8.cloned.1.call-start = ((), (), s32[]{:S(2)}) async-start(), calls=%async_computation.4 | async-start | bytes 2490368 | tf_op jit(solution)/shard_map/while/body/eval_jaxpr/psum | solution.py:55
  464.8 59.1 %copy-start.2 = (f32[36,128,128]{2,1,0:T(8,128)S(1)}, f32[36,128,128]{2,1,0:T(8,128)}, u32[]{:S(2)}) copy-start(f32[36,128,128]{2,1,0:T(8,128)} %all-gather.2.cloned.1.call-done) | copy-start | bytes 7077892 | tf_op jit(solution)/shard_map/while
  527.4 1.6 copy-start.3
  530.2 72.5 %reduce-scatter.2.cloned.1.call-start = ((), (), s32[]{:S(2)}) async-start(), calls=%async_computation.2 | async-start | bytes 2949120 | tf_op jit(solution)/shard_map/while/body/eval_jaxpr/reduce_scatter | solution.py:48
  559.6 74.3 %all-gather.2.cloned.1.call-start = ((), (), s32[]{:S(2)}) async-start(), calls=%async_computation.3 | async-start | bytes 2654208 | tf_op jit(solution)/shard_map/while/body/eval_jaxpr/all_gather | solution.py:49
  604.5 94.4 %all-reduce.8.cloned.1.call-start = ((), (), s32[]{:S(2)}) async-start(), calls=%async_computation.4 | async-start | bytes 2490368 | tf_op jit(solution)/shard_map/while/body/eval_jaxpr/psum | solution.py:55
  640.8 59.1 %copy-start.2 = (f32[36,128,128]{2,1,0:T(8,128)S(1)}, f32[36,128,128]{2,1,0:T(8,128)}, u32[]{:S(2)}) copy-start(f32[36,128,128]{2,1,0:T(8,128)} %all-gather.2.cloned.1.call-done) | copy-start | bytes 7077892 | tf_op jit(solution)/shard_map/while
  703.4 1.6 copy-start.3
  706.2 72.5 %reduce-scatter.2.cloned.1.call-start = ((), (), s32[]{:S(2)}) async-start(), calls=%async_computation.2 | async-start | bytes 2949120 | tf_op jit(solution)/shard_map/while/body/eval_jaxpr/reduce_scatter | solution.py:48
  735.6 74.3 %all-gather.2.cloned.1.call-start = ((), (), s32[]{:S(2)}) async-start(), calls=%async_computation.3 | async-start | bytes 2654208 | tf_op jit(solution)/shard_map/while/body/eval_jaxpr/all_gather | solution.py:49
  780.5 94.4 %all-reduce.8.cloned.1.call-start = ((), (), s32[]{:S(2)}) async-start(), calls=%async_computation.4 | async-start | bytes 2490368 | tf_op jit(solution)/shard_map/while/body/eval_jaxpr/psum | solution.py:55
  816.8 59.1 %copy-start.2 = (f32[36,128,128]{2,1,0:T(8,128)S(1)}, f32[36,128,128]{2,1,0:T(8,128)}, u32[]{:S(2)}) copy-start(f32[36,128,128]{2,1,0:T(8,128)} %all-gather.2.cloned.1.call-done) | copy-start | bytes 7077892 | tf_op jit(solution)/shard_map/while
  879.4 1.6 copy-start.3
  882.2 72.5 %reduce-scatter.2.cloned.1.call-start = ((), (), s32[]{:S(2)}) async-start(), calls=%async_computation.2 | async-start | bytes 2949120 | tf_op jit(solution)/shard_map/while/body/eval_jaxpr/reduce_scatter | solution.py:48
  911.5 74.3 %all-gather.2.cloned.1.call-start = ((), (), s32[]{:S(2)}) async-start(), calls=%async_computation.3 | async-start | bytes 2654208 | tf_op jit(solution)/shard_map/while/body/eval_jaxpr/all_gather | solution.py:49
  956.5 94.4 %all-reduce.8.cloned.1.call-start = ((), (), s32[]{:S(2)}) async-start(), calls=%async_computation.4 | async-start | bytes 2490368 | tf_op jit(solution)/shard_map/while/body/eval_jaxpr/psum | solution.py:55
  992.7 59.1 %copy-start.2 = (f32[36,128,128]{2,1,0:T(8,128)S(1)}, f32[36,128,128]{2,1,0:T(8,128)}, u32[]{:S(2)}) copy-start(f32[36,128,128]{2,1,0:T(8,128)} %all-gather.2.cloned.1.call-done) | copy-start | bytes 7077892 | tf_op jit(solution)/shard_map/while
  1055.3 1.6 copy-start.3
  1058.2 72.5 %reduce-scatter.2.cloned.1.call-start = ((), (), s32[]{:S(2)}) async-start(), calls=%async_computation.2 | async-start | bytes 2949120 | tf_op jit(solution)/shard_map/while/body/eval_jaxpr/reduce_scatter | solution.py:48
  1087.5 74.3 %all-gather.2.cloned.1.call-start = ((), (), s32[]{:S(2)}) async-start(), calls=%async_computation.3 | async-start | bytes 2654208 | tf_op jit(solution)/shard_map/while/body/eval_jaxpr/all_gather | solution.py:49
  1132.4 94.4 %all-reduce.8.cloned.1.call-start = ((), (), s32[]{:S(2)}) async-start(), calls=%async_computation.4 | async-start | bytes 2490368 | tf_op jit(solution)/shard_map/while/body/eval_jaxpr/psum | solution.py:55
  1168.7 59.1 %copy-start.2 = (f32[36,128,128]{2,1,0:T(8,128)S(1)}, f32[36,128,128]{2,1,0:T(8,128)}, u32[]{:S(2)}) copy-start(f32[36,128,128]{2,1,0:T(8,128)} %all-gather.2.cloned.1.call-done) | copy-start | bytes 7077892 | tf_op jit(solution)/shard_map/while
  1231.3 1.6 copy-start.3
  (1 other events, 0.9 us)
Sparse Core Ops, SparseCore 0:
  42.2 136.4 all-reduce.5
  208.2 42.5 reduce-scatter.1
  252.6 29.2 all-gather.1
  288.8 58.0 all-reduce.7
  383.7 42.9 reduce-scatter.1
  428.6 29.2 all-gather.1
  464.8 58.0 all-reduce.7
  559.7 42.9 reduce-scatter.1
  604.6 29.2 all-gather.1
  640.8 58.0 all-reduce.7
  735.7 42.9 reduce-scatter.1
  780.6 29.2 all-gather.1
  816.8 58.0 all-reduce.7
  911.6 42.9 reduce-scatter.1
  956.6 29.2 all-gather.1
  992.8 58.0 all-reduce.7
  1087.6 42.9 reduce-scatter.1
  1132.5 29.2 all-gather.1
  1168.7 58.0 all-reduce.7
where the time goes:
time: 1240 us
  waiting for transfers between devices  882 us (71%)
  matrix products  182 us (15%)
  local copies, waits for them, and re-layouts  101 us (8%)
  other arithmetic  62.3 us (5%)
  between operations  13.1 us (1%)
    psum x6, waiting for transfers between devices, advance(): diag_total = lax.psum(diag_term, 'prow')  328 us
    reduce_scatter x6, waiting for transfers between devices, advance(): lax.psum_scatter(partial_value, 'pcol', scatter_dimension=1, tiled=True)  258 us
    all_gather x6, waiting for transfers between devices, advance(): col_whole = lax.all_gather(col_piece, 'pcol', axis=1, tiled=True)  176 us
    dot_general x6, matrix products, advance(): jnp.einsum('acxy,cyz->axz', matrix, other_rows.astype(jnp.float32), preci...  162 us
    psum x1, waiting for transfers between devices, spread(): return lax.psum(kept, axis)  120 us
    unnamed x7, local copies, waits for them, and re-layouts  41.9 us
  transfers between devices with their start and end apart: 19, of which 19 were waited for; matrix products, arithmetic and copies ran while one was open for 3% of the time, Pallas kernels for 0%

commit v1 on v0

--- a/solution.py
+++ b/solution.py
@@ -46,7 +46,13 @@
             "acxy,cyz->axz", matrix, other_rows.astype(jnp.float32), precision=lax.Precision.HIGHEST
         )
         col_piece = lax.psum_scatter(partial_value, "pcol", scatter_dimension=1, tiled=True)
-        col_whole = lax.all_gather(col_piece, "pcol", axis=1, tiled=True)
+        size = lax.axis_size("pcol")
+        held, parts = (col_piece, [col_piece])
+        for _ in range(size - 1):
+            held = lax.ppermute(held, "pcol", [(i, (i + 1) % size) for i in range(size)])
+            parts.insert(0, held)
+        line = jnp.concatenate(parts, axis=1)
+        col_whole = jnp.roll(line, (lax.axis_index("pcol") + 1) * col_piece.shape[1], axis=1)
         live_rows = lax.dynamic_index_in_dim(mask_rows, column, 1, keepdims=False) > 0
         inverse_col = jnp.where(live_rows[:, None, None], col_whole, jnp.zeros_like(col_whole))
         diag_term = jnp.einsum(

time: 1240 us -> 1370 us (1.10)
  waiting for transfers between devices: 882 us -> 1010 us
    ppermute x0 -> x42, waiting for transfers between devices: none -> 296 us  [advance(): lax.ppermute(held, 'pcol', [(i, (i + 1) % size) for i in range(size)])]
    all_gather x6 -> x0, waiting for transfers between devices: 176 us -> none  [advance(): col_whole = lax.all_gather(col_piece, 'pcol', axis=1, tiled=True)]
  transfers between devices with their start and end apart: 19 -> 55, of which waited for: 19 -> 55; matrix products, arithmetic and copies ran while one was open for 3% -> 2% of each run, Pallas kernels for 0% -> 0%
where the time goes in v1:
time: 1370 us
  waiting for transfers between devices  1010 us (74%)
  matrix products  182 us (13%)
  local copies, waits for them, and re-layouts  109 us (8%)
  other arithmetic  53.8 us (4%)
    psum x6, waiting for transfers between devices, advance(): diag_total = lax.psum(diag_term, 'prow')  338 us
    ppermute x42, waiting for transfers between devices, advance(): lax.ppermute(held, 'pcol', [(i, (i + 1) % size) for i in range(size)])  296 us
    reduce_scatter x6, waiting for transfers between devices, advance(): lax.psum_scatter(partial_value, 'pcol', scatter_dimension=1, tiled=True)  258 us
    dot_general x6, matrix products, advance(): jnp.einsum('acxy,cyz->axz', matrix, other_rows.astype(jnp.float32), preci...  162 us
    psum x1, waiting for transfers between devices, spread(): return lax.psum(kept, axis)  120 us
    unnamed x7, local copies, waits for them, and re-layouts  42 us
  transfers between devices with their start and end apart: 55, of which 55 were waited for; matrix products, arithmetic and copies ran while one was open for 2% of the time, Pallas kernels for 0%

profile of v1, /device:TPU:0, one launch (start us, length us, event | category | flops | bytes accessed | tf_op | source)
XLA Modules:
  0.0 1372.0 jit_solution(9289342027818349833)
XLA Ops:
  6.5 30.5 %copy.104 = f32[36,1,18,1,128,128]{5,4,3,2,1,0:T(8,128)} copy(f32[36,1,18,1,128,128]{5,4,3,2,1,0:T(8,128)} %param.6) | data formatting | bytes 84934656
  42.3 10.4 copy.58
  59.1 119.6 %all-reduce.6.cloned.1.call-done = bf16[18,6,128,128]{3,2,1,0:T(8,128)(2,1)} async-done(((bf16[18,6,128,128]{3,2,1,0:T(8,128)(2,1)}), bf16[18,6,128,128]{3,2,1,0:T(8,128)(2,1)}) %all-reduce.6.cloned.1.call-update) | async-done | bytes 3538960 | tf_op jit(solution)/shard_map/psum | solution.py:9
  178.7 1185.9 %while.18 = (s32[]{:T(128)}, f32[36,18,128,128]{3,2,1,0:T(8,128)}, s32[]{:T(128)}, f32[6,128,128]{2,1,0:T(8,128)}, bf16[36,6,128,128]{2,3,0,1:T(8,128)(2,1)}, /*...) while((s32[]{:T(128)}, f32[36,18,128,128]{3,2,1,0:T(8,128)}, ...), condition=%wide.region_5.6_spmd.clone.clone, body=%wide.region_1.5_spmd.clone.clone.sunk | while | flops 17217585152 | bytes 140052240 | solution.py:82
  178.7 27.0 %fusion.32 = f32[36,128,128]{1,2,0:T(8,128)S(1)} fusion(f32[36,18,128,128]{3,2,1,0:T(8,128)} %get-tuple-element.579, bf16[18,6,128,128]{3,2,1,0:T(8,128)(2,1)} %get-tuple-element.613, s32[]{:T(128)S(6)} %select_n.424), kind=kOutput, calls=%fused_computation.6.clone.1 | convolution fusion | flops 16308043776 | bytes 45416452 | tf_op jit(solution)/shard_map/while/body/eval_jaxpr/acxy,cyz->axz/dot_general | solution.py:45
  208.0 42.6 %reduce-scatter.2.cloned.1.call-done = f32[36,16,128]{2,0,1:T(8,128)} async-done(((f32[36,128,128]{2,0,1:T(8,128)}), f32[36,16,128]{2,0,1:T(8,128)}) %reduce-scatter.2.cloned.1.call-update) | async-done | bytes 294928 | tf_op jit(solution)/shard_map/while/body/eval_jaxpr/reduce_scatter | solution.py:48
  272.9 7.0 collective-permute-done.3
  280.0 7.0 collective-permute-done.4
  310.6 56.2 %all-reduce.8.cloned.1.call-done = (f32[128,128]{1,0:T(8,128)}, f32[18,128,128]{2,1,0:T(8,128)}) async-done(((f32[128,128]{1,0:T(8,128)}, f32[18,128,128]{2,1,0:T(8,128)}), (f32[128,128]{1,0:T(8,128)}, f32[18,128,128]{2,1,0:T(8,128)})) %all-reduce.8.cloned.1.call-update) | async-done | bytes 1245200 | tf_op jit(solution)/shard_map/while/body/eval_jaxpr/psum | solution.py:61
  375.9 27.0 %fusion.32 = f32[36,128,128]{1,2,0:T(8,128)S(1)} fusion(f32[36,18,128,128]{3,2,1,0:T(8,128)} %get-tuple-element.579, bf16[18,6,128,128]{3,2,1,0:T(8,128)(2,1)} %get-tuple-element.613, s32[]{:T(128)S(6)} %select_n.424), kind=kOutput, calls=%fused_computation.6.clone.1 | convolution fusion | flops 16308043776 | bytes 45416452 | tf_op jit(solution)/shard_map/while/body/eval_jaxpr/acxy,cyz->axz/dot_general | solution.py:45
  405.2 43.1 %reduce-scatter.2.cloned.1.call-done = f32[36,16,128]{2,0,1:T(8,128)} async-done(((f32[36,128,128]{2,0,1:T(8,128)}), f32[36,16,128]{2,0,1:T(8,128)}) %reduce-scatter.2.cloned.1.call-update) | async-done | bytes 294928 | tf_op jit(solution)/shard_map/while/body/eval_jaxpr/reduce_scatter | solution.py:48
  456.5 7.0 collective-permute-done.1
  463.6 7.0 collective-permute-done.2
  484.7 7.0 collective-permute-done.5
  508.3 56.2 %all-reduce.8.cloned.1.call-done = (f32[128,128]{1,0:T(8,128)}, f32[18,128,128]{2,1,0:T(8,128)}) async-done(((f32[128,128]{1,0:T(8,128)}, f32[18,128,128]{2,1,0:T(8,128)}), (f32[128,128]{1,0:T(8,128)}, f32[18,128,128]{2,1,0:T(8,128)})) %all-reduce.8.cloned.1.call-update) | async-done | bytes 1245200 | tf_op jit(solution)/shard_map/while/body/eval_jaxpr/psum | solution.py:61
  573.6 27.0 %fusion.32 = f32[36,128,128]{1,2,0:T(8,128)S(1)} fusion(f32[36,18,128,128]{3,2,1,0:T(8,128)} %get-tuple-element.579, bf16[18,6,128,128]{3,2,1,0:T(8,128)(2,1)} %get-tuple-element.613, s32[]{:T(128)S(6)} %select_n.424), kind=kOutput, calls=%fused_computation.6.clone.1 | convolution fusion | flops 16308043776 | bytes 45416452 | tf_op jit(solution)/shard_map/while/body/eval_jaxpr/acxy,cyz->axz/dot_general | solution.py:45
  602.9 43.1 %reduce-scatter.2.cloned.1.call-done = f32[36,16,128]{2,0,1:T(8,128)} async-done(((f32[36,128,128]{2,0,1:T(8,128)}), f32[36,16,128]{2,0,1:T(8,128)}) %reduce-scatter.2.cloned.1.call-update) | async-done | bytes 294928 | tf_op jit(solution)/shard_map/while/body/eval_jaxpr/reduce_scatter | solution.py:48
  668.3 7.0 collective-permute-done.3
  675.4 7.0 collective-permute-done.4
  706.0 56.2 %all-reduce.8.cloned.1.call-done = (f32[128,128]{1,0:T(8,128)}, f32[18,128,128]{2,1,0:T(8,128)}) async-done(((f32[128,128]{1,0:T(8,128)}, f32[18,128,128]{2,1,0:T(8,128)}), (f32[128,128]{1,0:T(8,128)}, f32[18,128,128]{2,1,0:T(8,128)})) %all-reduce.8.cloned.1.call-update) | async-done | bytes 1245200 | tf_op jit(solution)/shard_map/while/body/eval_jaxpr/psum | solution.py:61
  771.3 27.1 %fusion.32 = f32[36,128,128]{1,2,0:T(8,128)S(1)} fusion(f32[36,18,128,128]{3,2,1,0:T(8,128)} %get-tuple-element.579, bf16[18,6,128,128]{3,2,1,0:T(8,128)(2,1)} %get-tuple-element.613, s32[]{:T(128)S(6)} %select_n.424), kind=kOutput, calls=%fused_computation.6.clone.1 | convolution fusion | flops 16308043776 | bytes 45416452 | tf_op jit(solution)/shard_map/while/body/eval_jaxpr/acxy,cyz->axz/dot_general | solution.py:45
  800.7 43.1 %reduce-scatter.2.cloned.1.call-done = f32[36,16,128]{2,0,1:T(8,128)} async-done(((f32[36,128,128]{2,0,1:T(8,128)}), f32[36,16,128]{2,0,1:T(8,128)}) %reduce-scatter.2.cloned.1.call-update) | async-done | bytes 294928 | tf_op jit(solution)/shard_map/while/body/eval_jaxpr/reduce_scatter | solution.py:48
  859.1 7.0 collective-permute-done.2
  866.1 7.0 collective-permute-done.3
  903.8 56.3 %all-reduce.8.cloned.1.call-done = (f32[128,128]{1,0:T(8,128)}, f32[18,128,128]{2,1,0:T(8,128)}) async-done(((f32[128,128]{1,0:T(8,128)}, f32[18,128,128]{2,1,0:T(8,128)}), (f32[128,128]{1,0:T(8,128)}, f32[18,128,128]{2,1,0:T(8,128)})) %all-reduce.8.cloned.1.call-update) | async-done | bytes 1245200 | tf_op jit(solution)/shard_map/while/body/eval_jaxpr/psum | solution.py:61
  969.1 27.0 %fusion.32 = f32[36,128,128]{1,2,0:T(8,128)S(1)} fusion(f32[36,18,128,128]{3,2,1,0:T(8,128)} %get-tuple-element.579, bf16[18,6,128,128]{3,2,1,0:T(8,128)(2,1)} %get-tuple-element.613, s32[]{:T(128)S(6)} %select_n.424), kind=kOutput, calls=%fused_computation.6.clone.1 | convolution fusion | flops 16308043776 | bytes 45416452 | tf_op jit(solution)/shard_map/while/body/eval_jaxpr/acxy,cyz->axz/dot_general | solution.py:45
  998.5 43.1 %reduce-scatter.2.cloned.1.call-done = f32[36,16,128]{2,0,1:T(8,128)} async-done(((f32[36,128,128]{2,0,1:T(8,128)}), f32[36,16,128]{2,0,1:T(8,128)}) %reduce-scatter.2.cloned.1.call-update) | async-done | bytes 294928 | tf_op jit(solution)/shard_map/while/body/eval_jaxpr/reduce_scatter | solution.py:48
  1049.8 7.0 collective-permute-done.1
  1101.6 56.2 %all-reduce.8.cloned.1.call-done = (f32[128,128]{1,0:T(8,128)}, f32[18,128,128]{2,1,0:T(8,128)}) async-done(((f32[128,128]{1,0:T(8,128)}, f32[18,128,128]{2,1,0:T(8,128)}), (f32[128,128]{1,0:T(8,128)}, f32[18,128,128]{2,1,0:T(8,128)})) %all-reduce.8.cloned.1.call-update) | async-done | bytes 1245200 | tf_op jit(solution)/shard_map/while/body/eval_jaxpr/psum | solution.py:61
  1166.9 27.0 %fusion.32 = f32[36,128,128]{1,2,0:T(8,128)S(1)} fusion(f32[36,18,128,128]{3,2,1,0:T(8,128)} %get-tuple-element.579, bf16[18,6,128,128]{3,2,1,0:T(8,128)(2,1)} %get-tuple-element.613, s32[]{:T(128)S(6)} %select_n.424), kind=kOutput, calls=%fused_computation.6.clone.1 | convolution fusion | flops 16308043776 | bytes 45416452 | tf_op jit(solution)/shard_map/while/body/eval_jaxpr/acxy,cyz->axz/dot_general | solution.py:45
  1196.2 43.1 %reduce-scatter.2.cloned.1.call-done = f32[36,16,128]{2,0,1:T(8,128)} async-done(((f32[36,128,128]{2,0,1:T(8,128)}), f32[36,16,128]{2,0,1:T(8,128)}) %reduce-scatter.2.cloned.1.call-update) | async-done | bytes 294928 | tf_op jit(solution)/shard_map/while/body/eval_jaxpr/reduce_scatter | solution.py:48
  1299.3 56.3 %all-reduce.8.cloned.1.call-done = (f32[128,128]{1,0:T(8,128)}, f32[18,128,128]{2,1,0:T(8,128)}) async-done(((f32[128,128]{1,0:T(8,128)}, f32[18,128,128]{2,1,0:T(8,128)}), (f32[128,128]{1,0:T(8,128)}, f32[18,128,128]{2,1,0:T(8,128)})) %all-reduce.8.cloned.1.call-update) | async-done | bytes 1245200 | tf_op jit(solution)/shard_map/while/body/eval_jaxpr/psum | solution.py:61
  (330 shorter events, 368.3 us)
Async XLA Ops:
  6.5 172.2 %all-reduce.6.cloned.1.call-start = ((), (), s32[]{:S(2)}) async-start(), calls=%async_computation.1 | async-start | bytes 7077888 | tf_op jit(solution)/shard_map/psum | solution.py:9
  178.7 71.9 %reduce-scatter.2.cloned.1.call-start = ((), (), s32[]{:S(2)}) async-start(), calls=%async_computation.2 | async-start | bytes 2949120 | tf_op jit(solution)/shard_map/while/body/eval_jaxpr/reduce_scatter | solution.py:48
  208.0 158.9 %all-reduce.8.cloned.1.call-start = ((), (), s32[]{:S(2)}) async-start(), calls=%async_computation.3 | async-start | bytes 2490368 | tf_op jit(solution)/shard_map/while/body/eval_jaxpr/psum | solution.py:61
  251.7 7.1 collective-permute-start
  272.9 7.0 collective-permute-start.3
  280.0 7.0 collective-permute-start.4
  375.9 72.4 %reduce-scatter.2.cloned.1.call-start = ((), (), s32[]{:S(2)}) async-start(), calls=%async_computation.2 | async-start | bytes 2949120 | tf_op jit(solution)/shard_map/while/body/eval_jaxpr/reduce_scatter | solution.py:48
  405.2 159.4 %all-reduce.8.cloned.1.call-start = ((), (), s32[]{:S(2)}) async-start(), calls=%async_computation.3 | async-start | bytes 2490368 | tf_op jit(solution)/shard_map/while/body/eval_jaxpr/psum | solution.py:61
  449.4 7.1 collective-permute-start
  456.5 7.0 collective-permute-start.1
  463.6 7.0 collective-permute-start.2
  484.7 7.0 collective-permute-start.5
  491.8 7.0 collective-permute-start.6
  573.6 72.4 %reduce-scatter.2.cloned.1.call-start = ((), (), s32[]{:S(2)}) async-start(), calls=%async_computation.2 | async-start | bytes 2949120 | tf_op jit(solution)/shard_map/while/body/eval_jaxpr/reduce_scatter | solution.py:48
  602.9 159.4 %all-reduce.8.cloned.1.call-start = ((), (), s32[]{:S(2)}) async-start(), calls=%async_computation.3 | async-start | bytes 2490368 | tf_op jit(solution)/shard_map/while/body/eval_jaxpr/psum | solution.py:61
  647.1 7.1 collective-permute-start
  668.3 7.0 collective-permute-start.3
  675.4 7.0 collective-permute-start.4
  771.3 72.6 %reduce-scatter.2.cloned.1.call-start = ((), (), s32[]{:S(2)}) async-start(), calls=%async_computation.2 | async-start | bytes 2949120 | tf_op jit(solution)/shard_map/while/body/eval_jaxpr/reduce_scatter | solution.py:48
  800.7 159.4 %all-reduce.8.cloned.1.call-start = ((), (), s32[]{:S(2)}) async-start(), calls=%async_computation.3 | async-start | bytes 2490368 | tf_op jit(solution)/shard_map/while/body/eval_jaxpr/psum | solution.py:61
  844.9 7.1 collective-permute-start
  866.1 7.0 collective-permute-start.3
  887.3 7.0 collective-permute-start.6
  969.1 72.4 %reduce-scatter.2.cloned.1.call-start = ((), (), s32[]{:S(2)}) async-start(), calls=%async_computation.2 | async-start | bytes 2949120 | tf_op jit(solution)/shard_map/while/body/eval_jaxpr/reduce_scatter | solution.py:48
  998.4 159.4 %all-reduce.8.cloned.1.call-start = ((), (), s32[]{:S(2)}) async-start(), calls=%async_computation.3 | async-start | bytes 2490368 | tf_op jit(solution)/shard_map/while/body/eval_jaxpr/psum | solution.py:61
  1042.7 7.1 collective-permute-start
  1049.8 7.0 collective-permute-start.1
  1078.0 7.0 collective-permute-start.5
  1166.9 72.4 %reduce-scatter.2.cloned.1.call-start = ((), (), s32[]{:S(2)}) async-start(), calls=%async_computation.2 | async-start | bytes 2949120 | tf_op jit(solution)/shard_map/while/body/eval_jaxpr/reduce_scatter | solution.py:48
  1196.1 159.4 %all-reduce.8.cloned.1.call-start = ((), (), s32[]{:S(2)}) async-start(), calls=%async_computation.3 | async-start | bytes 2490368 | tf_op jit(solution)/shard_map/while/body/eval_jaxpr/psum | solution.py:61
  1240.4 7.1 collective-permute-start
  1247.5 7.0 collective-permute-start.1
  (37 other events, 511.4 us)
Sparse Core Ops, SparseCore 0:
  42.2 136.4 all-reduce.5
  208.1 42.4 reduce-scatter.1
  308.8 58.0 all-reduce.7
  405.3 42.9 reduce-scatter.1
  506.5 58.0 all-reduce.7
  603.0 42.9 reduce-scatter.1
  704.2 58.0 all-reduce.7
  800.8 42.9 reduce-scatter.1
  902.0 58.0 all-reduce.7
  998.5 42.9 reduce-scatter.1
  1099.8 58.0 all-reduce.7
  1196.3 42.9 reduce-scatter.1
  1297.5 58.0 all-reduce.7
